TPU v7x, 256 devices: a whole 4x4x8 slice. The times are simulated.
256 devices in a mesh: epoch: 16 (over x, y), row: 16 (over z, core).
Axes of the slice: x: 4, y: 4, z: 8, core: 2. Of those that a mesh axis runs over, the one named last changes fastest.
Arguments:
- forcing: float32 [16, 2, 128, 6144], P('epoch', None, 'row'), may hold values from -2400 to 2400
- observed: float32 [16, 2, 128, 6144], P('epoch', None, 'row'), may hold values from -6 to 6
- log_friction: float32 [128, 6144], P('row'), may hold values from -1.5 to 1.5
- log_rheology: float32 [128, 6144], P('row'), may hold values from -0.7 to 0.7
- grounded: int32 [128, 6144], P('row'), may hold values 0 or 1
Outputs:
- new_friction: float32 [128, 6144], P('row')
- new_rheology: float32 [128, 6144], P('row')
All inputs are finite; a program needn't handle non-finite values. No bound on the sum of `grounded` on one device may be relied on, other than what follows from the above.
Results may differ from a plain program's by a relative error of at most 0.00011.
Values sent between devices are 32-bit elements; how exact they have to be, the bound alone decides.
A program may use at most 64 MiB of HBM per device.

v0:
```python
import jax
import jax.numpy as jnp
from jax import lax
from jax.sharding import PartitionSpec as P

SWEEPS = 4
relax = 0.9
coupling = 0.1
step_size = 0.5


def padded(x, sides, width):
    for axis, dim in sides:
        devices, length = (lax.axis_size(axis), x.shape[dim])
        up = [(i, (i + 1) % devices) for i in range(devices - 1)]
        down = [(j, i) for i, j in up]
        last = lax.slice_in_dim(x, length - width, length, axis=dim)
        first = lax.slice_in_dim(x, 0, width, axis=dim)
        before = lax.ppermute(last, axis, up)
        after = lax.ppermute(first, axis, down)
        x = jnp.concatenate([before, x, after], axis=dim)
    return x


def shift_east(field):
    widths = [(0, 0)] * (field.ndim - 1) + [(0, 1)]
    return jnp.pad(field[..., 1:], widths)


def shift_west(field):
    widths = [(0, 0)] * (field.ndim - 1) + [(1, 0)]
    return jnp.pad(field[..., :-1], widths)


def cross_term(padded_comp):
    return (
        shift_east(padded_comp[2:])
        - shift_west(padded_comp[2:])
        - shift_east(padded_comp[:-2])
        + shift_west(padded_comp[:-2])
    )


def jacobi_sweep(padded_velocity, padded_stiffness, friction_coef, forcing_now):
    centre = padded_stiffness[1:-1]
    face_east = 0.5 * (centre + shift_east(centre))
    face_west = 0.5 * (centre + shift_west(centre))
    face_north = 0.5 * (centre + padded_stiffness[:-2])
    face_south = 0.5 * (centre + padded_stiffness[2:])
    along_sum = face_east + face_west
    across = face_north + face_south
    diag_u = 4.0 * along_sum + across + friction_coef + 0.5
    diag_v = along_sum + 4.0 * across + friction_coef + 0.5
    padded_u = padded_velocity[0]
    padded_v = padded_velocity[1]
    inner_u = padded_u[1:-1]
    inner_v = padded_v[1:-1]
    lateral_u = face_east * shift_east(inner_u) + face_west * shift_west(inner_u)
    vertical_u = face_north * padded_u[:-2] + face_south * padded_u[2:]
    lateral_v = face_east * shift_east(inner_v) + face_west * shift_west(inner_v)
    vertical_v = face_north * padded_v[:-2] + face_south * padded_v[2:]
    image_u = (
        diag_u * inner_u - 4.0 * lateral_u - vertical_u - coupling * centre * cross_term(padded_v)
    )
    image_v = (
        diag_v * inner_v - lateral_v - 4.0 * vertical_v - coupling * centre * cross_term(padded_u)
    )
    new_u = inner_u + relax * (forcing_now[0] - image_u) / diag_u
    new_v = inner_v + relax * (forcing_now[1] - image_v) / diag_v
    return jnp.stack([new_u, new_v])


def on_device(forcing, observed, log_friction, log_rheology, grounded):
    forcing_now = forcing[0]
    target = observed[0]
    stiffness = jnp.exp(log_rheology)
    friction_coef = grounded.astype(jnp.float32) * jnp.exp(log_friction)
    row_count = stiffness.shape[0]
    padded_stiffness = padded(stiffness, (("row", 0),), 1)
    velocity = jnp.zeros(forcing_now.shape, jnp.float32)
    saved_states = []
    for sweep_index in range(SWEEPS):
        padded_velocity = padded(velocity, (("row", 1),), 1)
        saved_states.append(padded_velocity)
        velocity = jacobi_sweep(padded_velocity, padded_stiffness, friction_coef, forcing_now)
    adjoint = velocity - target
    stiff_back = jnp.zeros(padded_stiffness.shape, jnp.float32)
    friction_back = jnp.zeros(friction_coef.shape, jnp.float32)

    def local_sweep(padded_state, padded_stiff, friction_field):
        return jacobi_sweep(padded_state, padded_stiff, friction_field, forcing_now)

    for sweep_index in reversed(range(SWEEPS)):
        unused, pullback = jax.vjp(
            local_sweep, saved_states[sweep_index], padded_stiffness, friction_coef
        )
        state_back, stiff_part, friction_part = pullback(adjoint)
        stiff_back = stiff_back + stiff_part
        friction_back = friction_back + friction_part
        if sweep_index > 0:
            edge_rows = jnp.concatenate([state_back[:, :1], state_back[:, -1:]], axis=1)
            received = padded(edge_rows, (("row", 1),), 1)
            adjoint = (
                state_back[:, 1:-1]
                + jnp.pad(received[:, :1], ((0, 0), (0, row_count - 1), (0, 0)))
                + jnp.pad(received[:, 3:], ((0, 0), (row_count - 1, 0), (0, 0)))
            )
    stiff_edges = jnp.concatenate([stiff_back[:1], stiff_back[-1:]], axis=0)
    stiff_received = padded(stiff_edges, (("row", 0),), 1)
    grad_stiff = (
        stiff_back[1:-1]
        + jnp.pad(stiff_received[:1], ((0, row_count - 1), (0, 0)))
        + jnp.pad(stiff_received[3:], ((row_count - 1, 0), (0, 0)))
    )
    gradient = jnp.stack([friction_back * friction_coef, grad_stiff * stiffness])
    parameters = jnp.stack([log_friction, log_rheology])
    cell_count = row_count * lax.axis_size("row") * gradient.shape[2]
    summed = lax.psum(gradient, "epoch")
    squares = lax.psum(jnp.sum(summed * summed, axis=(1, 2)), "row")
    grad_scale = jnp.sqrt(squares / cell_count + 1e-06)
    updated = parameters - step_size * summed / grad_scale[:, None, None]
    return (updated[0], updated[1])


def solution(mesh):
    in_specs = (
        P("epoch", None, "row", None),
        P("epoch", None, "row", None),
        P("row", None),
        P("row", None),
        P("row", None),
    )
    out_specs = (P("row", None), P("row", None))
    return jax.shard_map(
        on_device, mesh=mesh, in_specs=in_specs, out_specs=out_specs, check_vma=False
    )
```

profile of v0, /device:TPU:1, one launch (start us, length us, event | category | flops | bytes accessed | tf_op | source)
XLA Modules:
  0.0 230.6 jit_solution(5686686242233176888)
XLA Ops:
  7.2 5.1 %collective-permute-start.3 = (f32[2,1,6144]{2,1,0:T(1,128)S(1)}, f32[2,1,6144]{2,1,0:T(1,128)S(1)}, u32[]{:S(2)}, u32[]{:S(2)}) collective-permute-start(f32[2,1,6144]{2,1,0:T(1,128)S(1)} %broadcast.392), channel_id=1, source_target_pairs={{1,0},{2,1},{3,2},{4,3},{5,4},{6,5},{7,6},{8,7},{9,8},{10,9},{11,1... | collective-permute-start | bytes 147464 | tf_op jit(solution)/shard_map/ppermute | solution.py:20
  12.4 1.9 collective-permute-start.2
  14.3 1.0 exp.6
  15.3 2.2 collective-permute-start
  17.5 2.1 collective-permute-start.1
  20.4 2.3 collective-permute-done.1
  23.7 1.9 collective-permute-start.5
  25.7 3.6 %collective-permute-start.4 = (f32[2,1,6144]{2,1,0:T(1,128)S(1)}, f32[2,1,6144]{2,1,0:T(1,128)S(1)}, u32[]{:S(2)}, u32[]{:S(2)}) collective-permute-start(f32[2,1,6144]{2,1,0:T(1,128)S(1)} %get-tuple-element.122), channel_id=1, source_target_pairs={{0,1},{1,2},{2,3},{3,4},{4,5},{5,6},{6,7},{7,8},{8,9},{9,10},{10,1... | collective-permute-start | bytes 147464 | tf_op jit(solution)/shard_map/ppermute | solution.py:19
  29.4 1.0 collective-permute-done.4
  31.9 1.9 collective-permute-start.7
  33.8 4.2 %collective-permute-start.6 = (f32[2,1,6144]{2,1,0:T(1,128)S(1)}, f32[2,1,6144]{2,1,0:T(1,128)S(1)}, u32[]{:S(2)}, u32[]{:S(2)}) collective-permute-start(f32[2,1,6144]{2,1,0:T(1,128)S(1)} %get-tuple-element.118), channel_id=1, source_target_pairs={{0,1},{1,2},{2,3},{3,4},{4,5},{5,6},{6,7},{7,8},{8,9},{9,10},{10,1... | collective-permute-start | bytes 147464 | tf_op jit(solution)/shard_map/ppermute | solution.py:19
  38.2 1.0 collective-permute-done.6
  40.7 4.2 %collective-permute-start.8 = (f32[2,1,6144]{2,1,0:T(1,128)S(1)}, f32[2,1,6144]{2,1,0:T(1,128)S(1)}, u32[]{:S(2)}, u32[]{:S(2)}) collective-permute-start(f32[2,1,6144]{2,1,0:T(1,128)S(1)} %get-tuple-element.113), channel_id=1, source_target_pairs={{0,1},{1,2},{2,3},{3,4},{4,5},{5,6},{6,7},{7,8},{8,9},{9,10},{10,1... | collective-permute-start | bytes 147464 | tf_op jit(solution)/shard_map/ppermute | solution.py:19
  45.0 1.9 collective-permute-start.9
  47.0 3.4 %collective-permute-done.9 = f32[2,1,6144]{2,1,0:T(1,128)S(1)} collective-permute-done((f32[2,1,6144]{2,1,0:T(1,128)S(1)}, f32[2,1,6144]{2,1,0:T(1,128)S(1)}, u32[]{:S(2)}, u32[]{:S(2)}) %collective-permute-start.9) | collective-permute-done | bytes 49184 | tf_op jit(solution)/shard_map/ppermute | solution.py:20
  54.2 1.9 collective-permute-start.10
  56.1 2.4 %collective-permute-start.11 = (f32[2,1,6144]{2,1,0:T(1,128)S(1)}, f32[2,1,6144]{2,1,0:T(1,128)S(1)}, u32[]{:S(2)}, u32[]{:S(2)}) collective-permute-start(f32[2,1,6144]{2,1,0:T(1,128)S(1)} %get-tuple-element.93), channel_id=1, source_target_pairs={{1,0},{2,1},{3,2},{4,3},{5,4},{6,5},{7,6},{8,7},{9,8},{10,9},{11,1... | collective-permute-start | bytes 147464 | tf_op jit(solution)/shard_map/ppermute | solution.py:20
  58.6 3.3 %collective-permute-done.11 = f32[2,1,6144]{2,1,0:T(1,128)S(1)} collective-permute-done((f32[2,1,6144]{2,1,0:T(1,128)S(1)}, f32[2,1,6144]{2,1,0:T(1,128)S(1)}, u32[]{:S(2)}, u32[]{:S(2)}) %collective-permute-start.11) | collective-permute-done | bytes 49184 | tf_op jit(solution)/shard_map/ppermute | solution.py:20
  63.8 1.9 collective-permute-start.12
  65.8 2.4 %collective-permute-start.13 = (f32[2,1,6144]{2,1,0:T(1,128)S(1)}, f32[2,1,6144]{2,1,0:T(1,128)S(1)}, u32[]{:S(2)}, u32[]{:S(2)}) collective-permute-start(f32[2,1,6144]{2,1,0:T(1,128)S(1)} %get-tuple-element.91), channel_id=1, source_target_pairs={{1,0},{2,1},{3,2},{4,3},{5,4},{6,5},{7,6},{8,7},{9,8},{10,9},{11,1... | collective-permute-start | bytes 147464 | tf_op jit(solution)/shard_map/ppermute | solution.py:20
  68.2 6.1 %collective-permute-done.13 = f32[2,1,6144]{2,1,0:T(1,128)S(1)} collective-permute-done((f32[2,1,6144]{2,1,0:T(1,128)S(1)}, f32[2,1,6144]{2,1,0:T(1,128)S(1)}, u32[]{:S(2)}, u32[]{:S(2)}) %collective-permute-start.13) | collective-permute-done | bytes 49184 | tf_op jit(solution)/shard_map/ppermute | solution.py:20
  76.3 2.3 %collective-permute-start.14 = (f32[2,1,6144]{2,1,0:T(1,128)S(1)}, f32[2,1,6144]{2,1,0:T(1,128)S(1)}, u32[]{:S(2)}, u32[]{:S(2)}) collective-permute-start(f32[2,1,6144]{2,1,0:T(1,128)S(1)} %get-tuple-element.88), channel_id=1, source_target_pairs={{0,1},{1,2},{2,3},{3,4},{4,5},{5,6},{6,7},{7,8},{8,9},{9,10},{10,1... | collective-permute-start | bytes 147464 | tf_op jit(solution)/shard_map/ppermute | solution.py:19
  78.6 2.2 collective-permute-start.15
  80.8 7.6 %collective-permute-done.15 = f32[2,1,6144]{2,1,0:T(1,128)S(1)} collective-permute-done((f32[2,1,6144]{2,1,0:T(1,128)S(1)}, f32[2,1,6144]{2,1,0:T(1,128)S(1)}, u32[]{:S(2)}, u32[]{:S(2)}) %collective-permute-start.15) | collective-permute-done | bytes 49184 | tf_op jit(solution)/shard_map/ppermute | solution.py:20
  91.2 1.9 collective-permute-start.16
  93.1 2.4 %collective-permute-start.17 = (f32[1,6144]{1,0:T(1,128)S(1)}, f32[1,6144]{1,0:T(1,128)S(1)}, u32[]{:S(2)}, u32[]{:S(2)}) collective-permute-start(f32[1,6144]{1,0:T(1,128)S(1)} %add_add_fusion.3), channel_id=1, source_target_pairs={{1,0},{2,1},{3,2},{4,3},{5,4},{6,5},{7,6},{8,7},{9,8},{10,9},{11,1... | collective-permute-start | bytes 73736 | tf_op jit(solution)/shard_map/ppermute | solution.py:20
  95.9 3.6 %collective-permute-done.17 = f32[1,6144]{1,0:T(1,128)S(1)} collective-permute-done((f32[1,6144]{1,0:T(1,128)S(1)}, f32[1,6144]{1,0:T(1,128)S(1)}, u32[]{:S(2)}, u32[]{:S(2)}) %collective-permute-start.17) | collective-permute-done | bytes 24608 | tf_op jit(solution)/shard_map/ppermute | solution.py:20
  99.5 0.8 pad_maximum_fusion
  100.4 95.9 %all-reduce.164.cloned.1.call-done = f32[2,8,6144]{2,1,0:T(8,128)} async-done(((f32[2,8,6144]{2,1,0:T(8,128)}), f32[2,8,6144]{2,1,0:T(8,128)}) %all-reduce.164.cloned.1.call-update) | async-done | bytes 393232 | tf_op jit(solution)/shard_map/psum | solution.py:118
  196.3 1.2 multiply_reduce_fusion
  197.5 25.3 %psum.15 = f32[2]{0:T(128)S(1)} all-reduce(f32[2]{0:T(128)S(1)} %multiply_reduce_fusion), channel_id=1, replica_groups=mesh['epoch'=16,'row'=16] {'row'}, use_global_device_ids=true, to_apply=%region_2.3 | all-reduce | flops 2 | bytes 16 | tf_op jit(solution)/shard_map/psum | solution.py:119
  223.0 0.8 slice_bitcast_fusion
  (130 shorter events, 15.7 us)
Async XLA Ops:
  7.2 189.2 %all-reduce.164.cloned.1.call-start = ((), (), s32[]{:S(2)}) async-start(), calls=%async_computation | async-start | bytes 786432 | tf_op jit(solution)/shard_map/psum | solution.py:118
  7.2 12.9 %collective-permute-start.3 = (f32[2,1,6144]{2,1,0:T(1,128)S(1)}, f32[2,1,6144]{2,1,0:T(1,128)S(1)}, u32[]{:S(2)}, u32[]{:S(2)}) collective-permute-start(f32[2,1,6144]{2,1,0:T(1,128)S(1)} %broadcast.392), channel_id=1, source_target_pairs={{1,0},{2,1},{3,2},{4,3},{5,4},{6,5},{7,6},{8,7},{9,8},{10,9},{11,1... | collective-permute-start | bytes 147464 | tf_op jit(solution)/shard_map/ppermute | solution.py:20
  12.4 7.5 %collective-permute-start.2 = (f32[2,1,6144]{2,1,0:T(1,128)S(1)}, f32[2,1,6144]{2,1,0:T(1,128)S(1)}, u32[]{:S(2)}, u32[]{:S(2)}) collective-permute-start(f32[2,1,6144]{2,1,0:T(1,128)S(1)} %broadcast.392), channel_id=1, source_target_pairs={{0,1},{1,2},{2,3},{3,4},{4,5},{5,6},{6,7},{7,8},{8,9},{9,10},{10,1... | collective-permute-start | bytes 147464 | tf_op jit(solution)/shard_map/ppermute | solution.py:19
  15.3 5.1 %collective-permute-start = (f32[1,6144]{1,0:T(1,128)S(1)}, f32[1,6144]{1,0:T(1,128)S(1)}, u32[]{:S(2)}, u32[]{:S(2)}) collective-permute-start(f32[1,6144]{1,0:T(1,128)S(1)} %get-tuple-element.211), channel_id=1, source_target_pairs={{0,1},{1,2},{2,3},{3,4},{4,5},{5,6},{6,7},{7,8},{8,9},{9,10},{10,1... | collective-permute-start | bytes 73736 | tf_op jit(solution)/shard_map/ppermute | solution.py:19
  17.5 5.1 %collective-permute-start.1 = (f32[1,6144]{1,0:T(1,128)S(1)}, f32[1,6144]{1,0:T(1,128)S(1)}, u32[]{:S(2)}, u32[]{:S(2)}) collective-permute-start(f32[1,6144]{1,0:T(1,128)S(1)} %get-tuple-element.212), channel_id=1, source_target_pairs={{1,0},{2,1},{3,2},{4,3},{5,4},{6,5},{7,6},{8,7},{9,8},{10,9},{11,1... | collective-permute-start | bytes 73736 | tf_op jit(solution)/shard_map/ppermute | solution.py:20
  20.2 2.5 %copy-start = (f32[8,6144]{1,0:T(8,128)S(1)}, f32[8,6144]{1,0:T(8,128)}, u32[]{:S(2)}) copy-start(f32[8,6144]{1,0:T(8,128)} %param.8) | copy-start | bytes 589828
  20.2 2.5 %copy-start.1 = (f32[1,2,8,6144]{3,2,1,0:T(8,128)S(1)}, f32[1,2,8,6144]{3,2,1,0:T(8,128)}, u32[]{:S(2)}) copy-start(f32[1,2,8,6144]{3,2,1,0:T(8,128)} %param.5) | copy-start | bytes 1179652
  20.2 2.5 %copy-start.2 = (f32[8,6144]{1,0:T(8,128)S(1)}, f32[8,6144]{1,0:T(8,128)}, u32[]{:S(2)}) copy-start(f32[8,6144]{1,0:T(8,128)} %param.7) | copy-start | bytes 589828
  20.2 2.5 %copy-start.3 = (s32[8,6144]{1,0:T(8,128)S(1)}, s32[8,6144]{1,0:T(8,128)}, u32[]{:S(2)}) copy-start(s32[8,6144]{1,0:T(8,128)} %param.9) | copy-start | bytes 589828
  23.7 5.7 %collective-permute-start.5 = (f32[2,1,6144]{2,1,0:T(1,128)S(1)}, f32[2,1,6144]{2,1,0:T(1,128)S(1)}, u32[]{:S(2)}, u32[]{:S(2)}) collective-permute-start(f32[2,1,6144]{2,1,0:T(1,128)S(1)} %get-tuple-element.121), channel_id=1, source_target_pairs={{1,0},{2,1},{3,2},{4,3},{5,4},{6,5},{7,6},{8,7},{9,8},{10,9},{11,1... | collective-permute-start | bytes 147464 | tf_op jit(solution)/shard_map/ppermute | solution.py:20
  25.7 4.8 %collective-permute-start.4 = (f32[2,1,6144]{2,1,0:T(1,128)S(1)}, f32[2,1,6144]{2,1,0:T(1,128)S(1)}, u32[]{:S(2)}, u32[]{:S(2)}) collective-permute-start(f32[2,1,6144]{2,1,0:T(1,128)S(1)} %get-tuple-element.122), channel_id=1, source_target_pairs={{0,1},{1,2},{2,3},{3,4},{4,5},{5,6},{6,7},{7,8},{8,9},{9,10},{10,1... | collective-permute-start | bytes 147464 | tf_op jit(solution)/shard_map/ppermute | solution.py:19
  31.9 6.3 %collective-permute-start.7 = (f32[2,1,6144]{2,1,0:T(1,128)S(1)}, f32[2,1,6144]{2,1,0:T(1,128)S(1)}, u32[]{:S(2)}, u32[]{:S(2)}) collective-permute-start(f32[2,1,6144]{2,1,0:T(1,128)S(1)} %get-tuple-element.117), channel_id=1, source_target_pairs={{1,0},{2,1},{3,2},{4,3},{5,4},{6,5},{7,6},{8,7},{9,8},{10,9},{11,1... | collective-permute-start | bytes 147464 | tf_op jit(solution)/shard_map/ppermute | solution.py:20
  33.8 5.4 %collective-permute-start.6 = (f32[2,1,6144]{2,1,0:T(1,128)S(1)}, f32[2,1,6144]{2,1,0:T(1,128)S(1)}, u32[]{:S(2)}, u32[]{:S(2)}) collective-permute-start(f32[2,1,6144]{2,1,0:T(1,128)S(1)} %get-tuple-element.118), channel_id=1, source_target_pairs={{0,1},{1,2},{2,3},{3,4},{4,5},{5,6},{6,7},{7,8},{8,9},{9,10},{10,1... | collective-permute-start | bytes 147464 | tf_op jit(solution)/shard_map/ppermute | solution.py:19
  40.7 6.3 %collective-permute-start.8 = (f32[2,1,6144]{2,1,0:T(1,128)S(1)}, f32[2,1,6144]{2,1,0:T(1,128)S(1)}, u32[]{:S(2)}, u32[]{:S(2)}) collective-permute-start(f32[2,1,6144]{2,1,0:T(1,128)S(1)} %get-tuple-element.113), channel_id=1, source_target_pairs={{0,1},{1,2},{2,3},{3,4},{4,5},{5,6},{6,7},{7,8},{8,9},{9,10},{10,1... | collective-permute-start | bytes 147464 | tf_op jit(solution)/shard_map/ppermute | solution.py:19
  45.0 5.4 %collective-permute-start.9 = (f32[2,1,6144]{2,1,0:T(1,128)S(1)}, f32[2,1,6144]{2,1,0:T(1,128)S(1)}, u32[]{:S(2)}, u32[]{:S(2)}) collective-permute-start(f32[2,1,6144]{2,1,0:T(1,128)S(1)} %get-tuple-element.114), channel_id=1, source_target_pairs={{1,0},{2,1},{3,2},{4,3},{5,4},{6,5},{7,6},{8,7},{9,8},{10,9},{11,1... | collective-permute-start | bytes 147464 | tf_op jit(solution)/shard_map/ppermute | solution.py:20
  51.3 1.0 copy-start.5
  54.2 4.3 %collective-permute-start.10 = (f32[2,1,6144]{2,1,0:T(1,128)S(1)}, f32[2,1,6144]{2,1,0:T(1,128)S(1)}, u32[]{:S(2)}, u32[]{:S(2)}) collective-permute-start(f32[2,1,6144]{2,1,0:T(1,128)S(1)} %get-tuple-element.92), channel_id=1, source_target_pairs={{0,1},{1,2},{2,3},{3,4},{4,5},{5,6},{6,7},{7,8},{8,9},{9,10},{10,1... | collective-permute-start | bytes 147464 | tf_op jit(solution)/shard_map/ppermute | solution.py:19
  56.1 5.7 %collective-permute-start.11 = (f32[2,1,6144]{2,1,0:T(1,128)S(1)}, f32[2,1,6144]{2,1,0:T(1,128)S(1)}, u32[]{:S(2)}, u32[]{:S(2)}) collective-permute-start(f32[2,1,6144]{2,1,0:T(1,128)S(1)} %get-tuple-element.93), channel_id=1, source_target_pairs={{1,0},{2,1},{3,2},{4,3},{5,4},{6,5},{7,6},{8,7},{9,8},{10,9},{11,1... | collective-permute-start | bytes 147464 | tf_op jit(solution)/shard_map/ppermute | solution.py:20
  63.8 4.3 %collective-permute-start.12 = (f32[2,1,6144]{2,1,0:T(1,128)S(1)}, f32[2,1,6144]{2,1,0:T(1,128)S(1)}, u32[]{:S(2)}, u32[]{:S(2)}) collective-permute-start(f32[2,1,6144]{2,1,0:T(1,128)S(1)} %get-tuple-element.90), channel_id=1, source_target_pairs={{0,1},{1,2},{2,3},{3,4},{4,5},{5,6},{6,7},{7,8},{8,9},{9,10},{10,1... | collective-permute-start | bytes 147464 | tf_op jit(solution)/shard_map/ppermute | solution.py:19
  65.8 8.5 %collective-permute-start.13 = (f32[2,1,6144]{2,1,0:T(1,128)S(1)}, f32[2,1,6144]{2,1,0:T(1,128)S(1)}, u32[]{:S(2)}, u32[]{:S(2)}) collective-permute-start(f32[2,1,6144]{2,1,0:T(1,128)S(1)} %get-tuple-element.91), channel_id=1, source_target_pairs={{1,0},{2,1},{3,2},{4,3},{5,4},{6,5},{7,6},{8,7},{9,8},{10,9},{11,1... | collective-permute-start | bytes 147464 | tf_op jit(solution)/shard_map/ppermute | solution.py:20
  76.3 4.5 %collective-permute-start.14 = (f32[2,1,6144]{2,1,0:T(1,128)S(1)}, f32[2,1,6144]{2,1,0:T(1,128)S(1)}, u32[]{:S(2)}, u32[]{:S(2)}) collective-permute-start(f32[2,1,6144]{2,1,0:T(1,128)S(1)} %get-tuple-element.88), channel_id=1, source_target_pairs={{0,1},{1,2},{2,3},{3,4},{4,5},{5,6},{6,7},{7,8},{8,9},{9,10},{10,1... | collective-permute-start | bytes 147464 | tf_op jit(solution)/shard_map/ppermute | solution.py:19
  78.6 9.8 %collective-permute-start.15 = (f32[2,1,6144]{2,1,0:T(1,128)S(1)}, f32[2,1,6144]{2,1,0:T(1,128)S(1)}, u32[]{:S(2)}, u32[]{:S(2)}) collective-permute-start(f32[2,1,6144]{2,1,0:T(1,128)S(1)} %get-tuple-element.89), channel_id=1, source_target_pairs={{1,0},{2,1},{3,2},{4,3},{5,4},{6,5},{7,6},{8,7},{9,8},{10,9},{11,1... | collective-permute-start | bytes 147464 | tf_op jit(solution)/shard_map/ppermute | solution.py:20
  91.2 4.7 %collective-permute-start.16 = (f32[1,6144]{1,0:T(1,128)S(1)}, f32[1,6144]{1,0:T(1,128)S(1)}, u32[]{:S(2)}, u32[]{:S(2)}) collective-permute-start(f32[1,6144]{1,0:T(1,128)S(1)} %add_add_fusion.4), channel_id=1, source_target_pairs={{0,1},{1,2},{2,3},{3,4},{4,5},{5,6},{6,7},{7,8},{8,9},{9,10},{10,1... | collective-permute-start | bytes 73736 | tf_op jit(solution)/shard_map/ppermute | solution.py:19
  93.1 6.4 %collective-permute-start.17 = (f32[1,6144]{1,0:T(1,128)S(1)}, f32[1,6144]{1,0:T(1,128)S(1)}, u32[]{:S(2)}, u32[]{:S(2)}) collective-permute-start(f32[1,6144]{1,0:T(1,128)S(1)} %add_add_fusion.3), channel_id=1, source_target_pairs={{1,0},{2,1},{3,2},{4,3},{5,4},{6,5},{7,6},{8,7},{9,8},{10,9},{11,1... | collective-permute-start | bytes 73736 | tf_op jit(solution)/shard_map/ppermute | solution.py:20
  196.3 26.5 %copy-start.4 = (f32[2,8,6144]{2,1,0:T(8,128)S(1)}, f32[2,8,6144]{2,1,0:T(8,128)}, u32[]{:S(2)}) copy-start(f32[2,8,6144]{2,1,0:T(8,128)} %all-reduce.164.cloned.1.call-done) | copy-start | bytes 1179652
Sparse Core Ops, SparseCore 0:
  100.5 95.7 all-reduce.163
where the time goes:
time: 231 us
  waiting for transfers between devices  124 us (54%)
  starting transfers between devices  46.8 us (20%)
  blocking collectives  25.3 us (11%)
  between operations  14.9 us (6%)
  other arithmetic  12.6 us (5%)
  local copies, waits for them, and re-layouts  6.81 us (3%)
    psum x1, waiting for transfers between devices, on_device(): summed = lax.psum(gradient, 'epoch')  95.9 us
    ppermute x9, waiting for transfers between devices, padded(): after = lax.ppermute(first, axis, down)  26.1 us
    psum x1, blocking collectives, on_device(): squares = lax.psum(jnp.sum(summed * summed, axis=(1, 2)), 'row')  25.3 us
    ppermute x9, starting transfers between devices, padded(): before = lax.ppermute(last, axis, up)  24.3 us
    ppermute x9, starting transfers between devices, padded(): after = lax.ppermute(first, axis, down)  22.4 us
  transfers between devices with their start and end apart: 19, of which 9 were waited for; matrix products, arithmetic and copies ran while one was open for 1% of the time, Pallas kernels for 0%

commit v1 on v0

--- a/solution.py
+++ b/solution.py
@@ -2,6 +2,7 @@
 import jax.numpy as jnp
 from jax import lax
 from jax.sharding import PartitionSpec as P
+from jax.lax import all_gather
 
 SWEEPS = 4
 relax = 0.9
@@ -115,7 +116,7 @@
     gradient = jnp.stack([friction_back * friction_coef, grad_stiff * stiffness])
     parameters = jnp.stack([log_friction, log_rheology])
     cell_count = row_count * lax.axis_size("row") * gradient.shape[2]
-    summed = lax.psum(gradient, "epoch")
+    summed = all_gather(gradient, "epoch").sum(axis=0)
     squares = lax.psum(jnp.sum(summed * summed, axis=(1, 2)), "row")
     grad_scale = jnp.sqrt(squares / cell_count + 1e-06)
     updated = parameters - step_size * summed / grad_scale[:, None, None]

time: 231 us -> 207 us (0.90)
  waiting for transfers between devices: 124 us -> 97.5 us
  other arithmetic: 12.6 us -> 15.5 us
    psum x1 -> x0, waiting for transfers between devices: 95.9 us -> none  [on_device(): summed = lax.psum(gradient, 'epoch')]
    all_gather x0 -> x1, waiting for transfers between devices: none -> 69.2 us  [on_device(): summed = all_gather(gradient, 'epoch').sum(axis=0)]
    reduce_sum x0 -> x1, other arithmetic: none -> 3.11 us  [on_device(): summed = all_gather(gradient, 'epoch').sum(axis=0)]
where the time goes in v1:
time: 207 us; the launch traced here: 205 us
  waiting for transfers between devices  97.5 us (47%)
  starting transfers between devices  47.1 us (23%)
  blocking collectives  24 us (12%)
  other arithmetic  15.5 us (7%)
  between operations  15 us (7%)
  local copies, waits for them, and re-layouts  6.16 us (3%)
    all_gather x1, waiting for transfers between devices, on_device(): summed = all_gather(gradient, 'epoch').sum(axis=0)  69.2 us
    ppermute x9, waiting for transfers between devices, padded(): after = lax.ppermute(first, axis, down)  26.2 us
    ppermute x9, starting transfers between devices, padded(): before = lax.ppermute(last, axis, up)  24.5 us
    psum x1, blocking collectives, on_device(): squares = lax.psum(jnp.sum(summed * summed, axis=(1, 2)), 'row')  24 us
    ppermute x9, starting transfers between devices, padded(): after = lax.ppermute(first, axis, down)  22.6 us
  transfers between devices with their start and end apart: 19, of which 9 were waited for; matrix products, arithmetic and copies ran while one was open for 1% of the time, Pallas kernels for 0%

profile of v1, /device:TPU:1, one launch (start us, length us, event | category | flops | bytes accessed | tf_op | source)
XLA Modules:
  0.0 205.2 jit_solution(14763147367769868228)
XLA Ops:
  7.3 5.3 %collective-permute-start.3 = (f32[2,1,6144]{2,1,0:T(1,128)S(1)}, f32[2,1,6144]{2,1,0:T(1,128)S(1)}, u32[]{:S(2)}, u32[]{:S(2)}) collective-permute-start(f32[2,1,6144]{2,1,0:T(1,128)S(1)} %broadcast.392), channel_id=1, source_target_pairs={{1,0},{2,1},{3,2},{4,3},{5,4},{6,5},{7,6},{8,7},{9,8},{10,9},{11,1... | collective-permute-start | bytes 147464 | tf_op jit(solution)/shard_map/ppermute | solution.py:21
  12.6 1.9 collective-permute-start.2
  14.5 1.0 exp.6
  15.5 2.2 %collective-permute-start = (f32[1,6144]{1,0:T(1,128)S(1)}, f32[1,6144]{1,0:T(1,128)S(1)}, u32[]{:S(2)}, u32[]{:S(2)}) collective-permute-start(f32[1,6144]{1,0:T(1,128)S(1)} %get-tuple-element.211), channel_id=1, source_target_pairs={{0,1},{1,2},{2,3},{3,4},{4,5},{5,6},{6,7},{7,8},{8,9},{9,10},{10,1... | collective-permute-start | bytes 73736 | tf_op jit(solution)/shard_map/ppermute | solution.py:20
  17.7 2.1 %collective-permute-start.1 = (f32[1,6144]{1,0:T(1,128)S(1)}, f32[1,6144]{1,0:T(1,128)S(1)}, u32[]{:S(2)}, u32[]{:S(2)}) collective-permute-start(f32[1,6144]{1,0:T(1,128)S(1)} %get-tuple-element.212), channel_id=1, source_target_pairs={{1,0},{2,1},{3,2},{4,3},{5,4},{6,5},{7,6},{8,7},{9,8},{10,9},{11,1... | collective-permute-start | bytes 73736 | tf_op jit(solution)/shard_map/ppermute | solution.py:21
  20.5 2.3 %collective-permute-done.1 = f32[1,6144]{1,0:T(1,128)S(1)} collective-permute-done((f32[1,6144]{1,0:T(1,128)S(1)}, f32[1,6144]{1,0:T(1,128)S(1)}, u32[]{:S(2)}, u32[]{:S(2)}) %collective-permute-start.1) | collective-permute-done | bytes 24608 | tf_op jit(solution)/shard_map/ppermute | solution.py:21
  22.8 1.6 fusion.115
  25.1 1.9 collective-permute-start.5
  27.0 3.6 %collective-permute-start.4 = (f32[2,1,6144]{2,1,0:T(1,128)S(1)}, f32[2,1,6144]{2,1,0:T(1,128)S(1)}, u32[]{:S(2)}, u32[]{:S(2)}) collective-permute-start(f32[2,1,6144]{2,1,0:T(1,128)S(1)} %get-tuple-element.122), channel_id=1, source_target_pairs={{0,1},{1,2},{2,3},{3,4},{4,5},{5,6},{6,7},{7,8},{8,9},{9,10},{10,1... | collective-permute-start | bytes 147464 | tf_op jit(solution)/shard_map/ppermute | solution.py:20
  30.8 1.0 collective-permute-done.4
  33.2 1.9 collective-permute-start.7
  35.2 4.2 %collective-permute-start.6 = (f32[2,1,6144]{2,1,0:T(1,128)S(1)}, f32[2,1,6144]{2,1,0:T(1,128)S(1)}, u32[]{:S(2)}, u32[]{:S(2)}) collective-permute-start(f32[2,1,6144]{2,1,0:T(1,128)S(1)} %get-tuple-element.118), channel_id=1, source_target_pairs={{0,1},{1,2},{2,3},{3,4},{4,5},{5,6},{6,7},{7,8},{8,9},{9,10},{10,1... | collective-permute-start | bytes 147464 | tf_op jit(solution)/shard_map/ppermute | solution.py:20
  39.5 1.0 collective-permute-done.6
  42.0 4.4 %collective-permute-start.8 = (f32[2,1,6144]{2,1,0:T(1,128)S(1)}, f32[2,1,6144]{2,1,0:T(1,128)S(1)}, u32[]{:S(2)}, u32[]{:S(2)}) collective-permute-start(f32[2,1,6144]{2,1,0:T(1,128)S(1)} %get-tuple-element.113), channel_id=1, source_target_pairs={{0,1},{1,2},{2,3},{3,4},{4,5},{5,6},{6,7},{7,8},{8,9},{9,10},{10,1... | collective-permute-start | bytes 147464 | tf_op jit(solution)/shard_map/ppermute | solution.py:20
  46.4 1.9 collective-permute-start.9
  48.4 3.4 %collective-permute-done.9 = f32[2,1,6144]{2,1,0:T(1,128)S(1)} collective-permute-done((f32[2,1,6144]{2,1,0:T(1,128)S(1)}, f32[2,1,6144]{2,1,0:T(1,128)S(1)}, u32[]{:S(2)}, u32[]{:S(2)}) %collective-permute-start.9) | collective-permute-done | bytes 49184 | tf_op jit(solution)/shard_map/ppermute | solution.py:21
  54.9 1.9 collective-permute-start.10
  56.9 2.4 %collective-permute-start.11 = (f32[2,1,6144]{2,1,0:T(1,128)S(1)}, f32[2,1,6144]{2,1,0:T(1,128)S(1)}, u32[]{:S(2)}, u32[]{:S(2)}) collective-permute-start(f32[2,1,6144]{2,1,0:T(1,128)S(1)} %get-tuple-element.93), channel_id=1, source_target_pairs={{1,0},{2,1},{3,2},{4,3},{5,4},{6,5},{7,6},{8,7},{9,8},{10,9},{11,1... | collective-permute-start | bytes 147464 | tf_op jit(solution)/shard_map/ppermute | solution.py:21
  59.3 3.3 %collective-permute-done.11 = f32[2,1,6144]{2,1,0:T(1,128)S(1)} collective-permute-done((f32[2,1,6144]{2,1,0:T(1,128)S(1)}, f32[2,1,6144]{2,1,0:T(1,128)S(1)}, u32[]{:S(2)}, u32[]{:S(2)}) %collective-permute-start.11) | collective-permute-done | bytes 49184 | tf_op jit(solution)/shard_map/ppermute | solution.py:21
  64.5 1.9 collective-permute-start.12
  66.5 2.4 %collective-permute-start.13 = (f32[2,1,6144]{2,1,0:T(1,128)S(1)}, f32[2,1,6144]{2,1,0:T(1,128)S(1)}, u32[]{:S(2)}, u32[]{:S(2)}) collective-permute-start(f32[2,1,6144]{2,1,0:T(1,128)S(1)} %get-tuple-element.91), channel_id=1, source_target_pairs={{1,0},{2,1},{3,2},{4,3},{5,4},{6,5},{7,6},{8,7},{9,8},{10,9},{11,1... | collective-permute-start | bytes 147464 | tf_op jit(solution)/shard_map/ppermute | solution.py:21
  68.9 6.1 %collective-permute-done.13 = f32[2,1,6144]{2,1,0:T(1,128)S(1)} collective-permute-done((f32[2,1,6144]{2,1,0:T(1,128)S(1)}, f32[2,1,6144]{2,1,0:T(1,128)S(1)}, u32[]{:S(2)}, u32[]{:S(2)}) %collective-permute-start.13) | collective-permute-done | bytes 49184 | tf_op jit(solution)/shard_map/ppermute | solution.py:21
  76.9 2.3 %collective-permute-start.14 = (f32[2,1,6144]{2,1,0:T(1,128)S(1)}, f32[2,1,6144]{2,1,0:T(1,128)S(1)}, u32[]{:S(2)}, u32[]{:S(2)}) collective-permute-start(f32[2,1,6144]{2,1,0:T(1,128)S(1)} %get-tuple-element.88), channel_id=1, source_target_pairs={{0,1},{1,2},{2,3},{3,4},{4,5},{5,6},{6,7},{7,8},{8,9},{9,10},{10,1... | collective-permute-start | bytes 147464 | tf_op jit(solution)/shard_map/ppermute | solution.py:20
  79.3 2.2 %collective-permute-start.15 = (f32[2,1,6144]{2,1,0:T(1,128)S(1)}, f32[2,1,6144]{2,1,0:T(1,128)S(1)}, u32[]{:S(2)}, u32[]{:S(2)}) collective-permute-start(f32[2,1,6144]{2,1,0:T(1,128)S(1)} %get-tuple-element.89), channel_id=1, source_target_pairs={{1,0},{2,1},{3,2},{4,3},{5,4},{6,5},{7,6},{8,7},{9,8},{10,9},{11,1... | collective-permute-start | bytes 147464 | tf_op jit(solution)/shard_map/ppermute | solution.py:21
  81.5 7.6 %collective-permute-done.15 = f32[2,1,6144]{2,1,0:T(1,128)S(1)} collective-permute-done((f32[2,1,6144]{2,1,0:T(1,128)S(1)}, f32[2,1,6144]{2,1,0:T(1,128)S(1)}, u32[]{:S(2)}, u32[]{:S(2)}) %collective-permute-start.15) | collective-permute-done | bytes 49184 | tf_op jit(solution)/shard_map/ppermute | solution.py:21
  91.8 1.9 collective-permute-start.16
  93.7 2.4 %collective-permute-start.17 = (f32[1,6144]{1,0:T(1,128)S(1)}, f32[1,6144]{1,0:T(1,128)S(1)}, u32[]{:S(2)}, u32[]{:S(2)}) collective-permute-start(f32[1,6144]{1,0:T(1,128)S(1)} %add_add_fusion.3), channel_id=1, source_target_pairs={{1,0},{2,1},{3,2},{4,3},{5,4},{6,5},{7,6},{8,7},{9,8},{10,9},{11,1... | collective-permute-start | bytes 73736 | tf_op jit(solution)/shard_map/ppermute | solution.py:21
  96.5 3.6 %collective-permute-done.17 = f32[1,6144]{1,0:T(1,128)S(1)} collective-permute-done((f32[1,6144]{1,0:T(1,128)S(1)}, f32[1,6144]{1,0:T(1,128)S(1)}, u32[]{:S(2)}, u32[]{:S(2)}) %collective-permute-start.17) | collective-permute-done | bytes 24608 | tf_op jit(solution)/shard_map/ppermute | solution.py:21
  100.2 0.8 pad_maximum_fusion
  101.0 69.2 %all-gather.3.cloned.1.call-done = f32[32,8,6144]{2,1,0:T(8,128)} async-done(((f32[2,8,6144]{2,1,0:T(8,128)}), f32[32,8,6144]{2,1,0:T(8,128)}) %all-gather.3.cloned.1.call-update) | async-done | bytes 6291472 | tf_op jit(solution)/shard_map/all_gather | solution.py:119
  170.1 3.1 %reduce_sum.18 = f32[2,8,6144]{2,1,0:T(8,128)S(1)} reduce(f32[16,2,8,6144]{3,2,1,0:T(8,128)} %bitcast.230, f32[]{:T(128)} %constant.68.clone.1), dimensions={0}, to_apply=%region_0.1 | reduce | flops 1474560 | bytes 6684676 | tf_op jit(solution)/shard_map/reduce_sum | solution.py:119
  173.4 24.0 %psum.7 = f32[2]{0:T(128)S(1)} all-reduce(f32[2]{0:T(128)S(1)} %multiply_reduce_fusion), channel_id=1, replica_groups=mesh['epoch'=16,'row'=16] {'row'}, use_global_device_ids=true, to_apply=%region_2.3 | all-reduce | flops 2 | bytes 16 | tf_op jit(solution)/shard_map/psum | solution.py:120
  (129 shorter events, 15.2 us)
Async XLA Ops:
  7.2 17.4 %copy-start.1 = (f32[1,2,8,6144]{3,2,1,0:T(8,128)S(1)}, f32[1,2,8,6144]{3,2,1,0:T(8,128)}, u32[]{:S(2)}) copy-start(f32[1,2,8,6144]{3,2,1,0:T(8,128)} %param.5) | copy-start | bytes 1179652
  7.2 17.4 %copy-start.2 = (f32[8,6144]{1,0:T(8,128)S(1)}, f32[8,6144]{1,0:T(8,128)}, u32[]{:S(2)}) copy-start(f32[8,6144]{1,0:T(8,128)} %param.7) | copy-start | bytes 589828
  7.2 17.4 %copy-start.3 = (s32[8,6144]{1,0:T(8,128)S(1)}, s32[8,6144]{1,0:T(8,128)}, u32[]{:S(2)}) copy-start(s32[8,6144]{1,0:T(8,128)} %param.9) | copy-start | bytes 589828
  7.2 162.9 %all-gather.3.cloned.1.call-start = ((), (), s32[]{:S(2)}) async-start(), calls=%async_computation | async-start | bytes 6684672 | tf_op jit(solution)/shard_map/all_gather | solution.py:119
  7.3 13.0 %collective-permute-start.3 = (f32[2,1,6144]{2,1,0:T(1,128)S(1)}, f32[2,1,6144]{2,1,0:T(1,128)S(1)}, u32[]{:S(2)}, u32[]{:S(2)}) collective-permute-start(f32[2,1,6144]{2,1,0:T(1,128)S(1)} %broadcast.392), channel_id=1, source_target_pairs={{1,0},{2,1},{3,2},{4,3},{5,4},{6,5},{7,6},{8,7},{9,8},{10,9},{11,1... | collective-permute-start | bytes 147464 | tf_op jit(solution)/shard_map/ppermute | solution.py:21
  12.6 7.5 %collective-permute-start.2 = (f32[2,1,6144]{2,1,0:T(1,128)S(1)}, f32[2,1,6144]{2,1,0:T(1,128)S(1)}, u32[]{:S(2)}, u32[]{:S(2)}) collective-permute-start(f32[2,1,6144]{2,1,0:T(1,128)S(1)} %broadcast.392), channel_id=1, source_target_pairs={{0,1},{1,2},{2,3},{3,4},{4,5},{5,6},{6,7},{7,8},{8,9},{9,10},{10,1... | collective-permute-start | bytes 147464 | tf_op jit(solution)/shard_map/ppermute | solution.py:20
  15.5 5.0 %collective-permute-start = (f32[1,6144]{1,0:T(1,128)S(1)}, f32[1,6144]{1,0:T(1,128)S(1)}, u32[]{:S(2)}, u32[]{:S(2)}) collective-permute-start(f32[1,6144]{1,0:T(1,128)S(1)} %get-tuple-element.211), channel_id=1, source_target_pairs={{0,1},{1,2},{2,3},{3,4},{4,5},{5,6},{6,7},{7,8},{8,9},{9,10},{10,1... | collective-permute-start | bytes 73736 | tf_op jit(solution)/shard_map/ppermute | solution.py:20
  17.7 5.1 %collective-permute-start.1 = (f32[1,6144]{1,0:T(1,128)S(1)}, f32[1,6144]{1,0:T(1,128)S(1)}, u32[]{:S(2)}, u32[]{:S(2)}) collective-permute-start(f32[1,6144]{1,0:T(1,128)S(1)} %get-tuple-element.212), channel_id=1, source_target_pairs={{1,0},{2,1},{3,2},{4,3},{5,4},{6,5},{7,6},{8,7},{9,8},{10,9},{11,1... | collective-permute-start | bytes 73736 | tf_op jit(solution)/shard_map/ppermute | solution.py:21
  25.1 5.7 %collective-permute-start.5 = (f32[2,1,6144]{2,1,0:T(1,128)S(1)}, f32[2,1,6144]{2,1,0:T(1,128)S(1)}, u32[]{:S(2)}, u32[]{:S(2)}) collective-permute-start(f32[2,1,6144]{2,1,0:T(1,128)S(1)} %get-tuple-element.121), channel_id=1, source_target_pairs={{1,0},{2,1},{3,2},{4,3},{5,4},{6,5},{7,6},{8,7},{9,8},{10,9},{11,1... | collective-permute-start | bytes 147464 | tf_op jit(solution)/shard_map/ppermute | solution.py:21
  27.0 4.8 %collective-permute-start.4 = (f32[2,1,6144]{2,1,0:T(1,128)S(1)}, f32[2,1,6144]{2,1,0:T(1,128)S(1)}, u32[]{:S(2)}, u32[]{:S(2)}) collective-permute-start(f32[2,1,6144]{2,1,0:T(1,128)S(1)} %get-tuple-element.122), channel_id=1, source_target_pairs={{0,1},{1,2},{2,3},{3,4},{4,5},{5,6},{6,7},{7,8},{8,9},{9,10},{10,1... | collective-permute-start | bytes 147464 | tf_op jit(solution)/shard_map/ppermute | solution.py:20
  33.2 6.3 %collective-permute-start.7 = (f32[2,1,6144]{2,1,0:T(1,128)S(1)}, f32[2,1,6144]{2,1,0:T(1,128)S(1)}, u32[]{:S(2)}, u32[]{:S(2)}) collective-permute-start(f32[2,1,6144]{2,1,0:T(1,128)S(1)} %get-tuple-element.117), channel_id=1, source_target_pairs={{1,0},{2,1},{3,2},{4,3},{5,4},{6,5},{7,6},{8,7},{9,8},{10,9},{11,1... | collective-permute-start | bytes 147464 | tf_op jit(solution)/shard_map/ppermute | solution.py:21
  35.2 5.4 %collective-permute-start.6 = (f32[2,1,6144]{2,1,0:T(1,128)S(1)}, f32[2,1,6144]{2,1,0:T(1,128)S(1)}, u32[]{:S(2)}, u32[]{:S(2)}) collective-permute-start(f32[2,1,6144]{2,1,0:T(1,128)S(1)} %get-tuple-element.118), channel_id=1, source_target_pairs={{0,1},{1,2},{2,3},{3,4},{4,5},{5,6},{6,7},{7,8},{8,9},{9,10},{10,1... | collective-permute-start | bytes 147464 | tf_op jit(solution)/shard_map/ppermute | solution.py:20
  41.9 11.1 %copy-start.4 = (f32[1,2,8,6144]{3,2,1,0:T(8,128)S(1)}, f32[1,2,8,6144]{3,2,1,0:T(8,128)}, u32[]{:S(2)}) copy-start(f32[1,2,8,6144]{3,2,1,0:T(8,128)} %param.6) | copy-start | bytes 1179652
  42.0 6.4 %collective-permute-start.8 = (f32[2,1,6144]{2,1,0:T(1,128)S(1)}, f32[2,1,6144]{2,1,0:T(1,128)S(1)}, u32[]{:S(2)}, u32[]{:S(2)}) collective-permute-start(f32[2,1,6144]{2,1,0:T(1,128)S(1)} %get-tuple-element.113), channel_id=1, source_target_pairs={{0,1},{1,2},{2,3},{3,4},{4,5},{5,6},{6,7},{7,8},{8,9},{9,10},{10,1... | collective-permute-start | bytes 147464 | tf_op jit(solution)/shard_map/ppermute | solution.py:20
  46.4 5.4 %collective-permute-start.9 = (f32[2,1,6144]{2,1,0:T(1,128)S(1)}, f32[2,1,6144]{2,1,0:T(1,128)S(1)}, u32[]{:S(2)}, u32[]{:S(2)}) collective-permute-start(f32[2,1,6144]{2,1,0:T(1,128)S(1)} %get-tuple-element.114), channel_id=1, source_target_pairs={{1,0},{2,1},{3,2},{4,3},{5,4},{6,5},{7,6},{8,7},{9,8},{10,9},{11,1... | collective-permute-start | bytes 147464 | tf_op jit(solution)/shard_map/ppermute | solution.py:21
  52.1 1.3 copy-start
  54.9 4.3 %collective-permute-start.10 = (f32[2,1,6144]{2,1,0:T(1,128)S(1)}, f32[2,1,6144]{2,1,0:T(1,128)S(1)}, u32[]{:S(2)}, u32[]{:S(2)}) collective-permute-start(f32[2,1,6144]{2,1,0:T(1,128)S(1)} %get-tuple-element.92), channel_id=1, source_target_pairs={{0,1},{1,2},{2,3},{3,4},{4,5},{5,6},{6,7},{7,8},{8,9},{9,10},{10,1... | collective-permute-start | bytes 147464 | tf_op jit(solution)/shard_map/ppermute | solution.py:20
  56.9 5.7 %collective-permute-start.11 = (f32[2,1,6144]{2,1,0:T(1,128)S(1)}, f32[2,1,6144]{2,1,0:T(1,128)S(1)}, u32[]{:S(2)}, u32[]{:S(2)}) collective-permute-start(f32[2,1,6144]{2,1,0:T(1,128)S(1)} %get-tuple-element.93), channel_id=1, source_target_pairs={{1,0},{2,1},{3,2},{4,3},{5,4},{6,5},{7,6},{8,7},{9,8},{10,9},{11,1... | collective-permute-start | bytes 147464 | tf_op jit(solution)/shard_map/ppermute | solution.py:21
  64.5 4.3 %collective-permute-start.12 = (f32[2,1,6144]{2,1,0:T(1,128)S(1)}, f32[2,1,6144]{2,1,0:T(1,128)S(1)}, u32[]{:S(2)}, u32[]{:S(2)}) collective-permute-start(f32[2,1,6144]{2,1,0:T(1,128)S(1)} %get-tuple-element.90), channel_id=1, source_target_pairs={{0,1},{1,2},{2,3},{3,4},{4,5},{5,6},{6,7},{7,8},{8,9},{9,10},{10,1... | collective-permute-start | bytes 147464 | tf_op jit(solution)/shard_map/ppermute | solution.py:20
  66.5 8.5 %collective-permute-start.13 = (f32[2,1,6144]{2,1,0:T(1,128)S(1)}, f32[2,1,6144]{2,1,0:T(1,128)S(1)}, u32[]{:S(2)}, u32[]{:S(2)}) collective-permute-start(f32[2,1,6144]{2,1,0:T(1,128)S(1)} %get-tuple-element.91), channel_id=1, source_target_pairs={{1,0},{2,1},{3,2},{4,3},{5,4},{6,5},{7,6},{8,7},{9,8},{10,9},{11,1... | collective-permute-start | bytes 147464 | tf_op jit(solution)/shard_map/ppermute | solution.py:21
  76.9 4.5 %collective-permute-start.14 = (f32[2,1,6144]{2,1,0:T(1,128)S(1)}, f32[2,1,6144]{2,1,0:T(1,128)S(1)}, u32[]{:S(2)}, u32[]{:S(2)}) collective-permute-start(f32[2,1,6144]{2,1,0:T(1,128)S(1)} %get-tuple-element.88), channel_id=1, source_target_pairs={{0,1},{1,2},{2,3},{3,4},{4,5},{5,6},{6,7},{7,8},{8,9},{9,10},{10,1... | collective-permute-start | bytes 147464 | tf_op jit(solution)/shard_map/ppermute | solution.py:20
  79.3 9.8 %collective-permute-start.15 = (f32[2,1,6144]{2,1,0:T(1,128)S(1)}, f32[2,1,6144]{2,1,0:T(1,128)S(1)}, u32[]{:S(2)}, u32[]{:S(2)}) collective-permute-start(f32[2,1,6144]{2,1,0:T(1,128)S(1)} %get-tuple-element.89), channel_id=1, source_target_pairs={{1,0},{2,1},{3,2},{4,3},{5,4},{6,5},{7,6},{8,7},{9,8},{10,9},{11,1... | collective-permute-start | bytes 147464 | tf_op jit(solution)/shard_map/ppermute | solution.py:21
  91.8 4.7 %collective-permute-start.16 = (f32[1,6144]{1,0:T(1,128)S(1)}, f32[1,6144]{1,0:T(1,128)S(1)}, u32[]{:S(2)}, u32[]{:S(2)}) collective-permute-start(f32[1,6144]{1,0:T(1,128)S(1)} %add_add_fusion.4), channel_id=1, source_target_pairs={{0,1},{1,2},{2,3},{3,4},{4,5},{5,6},{6,7},{7,8},{8,9},{9,10},{10,1... | collective-permute-start | bytes 73736 | tf_op jit(solution)/shard_map/ppermute | solution.py:20
  93.7 6.4 %collective-permute-start.17 = (f32[1,6144]{1,0:T(1,128)S(1)}, f32[1,6144]{1,0:T(1,128)S(1)}, u32[]{:S(2)}, u32[]{:S(2)}) collective-permute-start(f32[1,6144]{1,0:T(1,128)S(1)} %add_add_fusion.3), channel_id=1, source_target_pairs={{1,0},{2,1},{3,2},{4,3},{5,4},{6,5},{7,6},{8,7},{9,8},{10,9},{11,1... | collective-permute-start | bytes 73736 | tf_op jit(solution)/shard_map/ppermute | solution.py:21
Sparse Core Ops, SparseCore 0:
  101.1 69.0 all-gather.2
